TPU v7x, 32 devices: a whole 2x2x4 slice. The times are simulated.
32 devices in a mesh: dp: 8 (over y, x, core), ctx: 4 (over z).
Axes of the slice: x: 2, y: 2, z: 4, core: 2. Of those that a mesh axis runs over, the one named last changes fastest.
Arguments:
- hidden_in: float32 [8, 512, 960], P('dp', 'ctx'), may hold values from -6 to 6
- segments: int32 [8, 512], P('dp'), may hold values from 0 to 3, never falling along the last dimension, each value on 1 to 256 neighbouring positions
- attn_flat: bfloat16 [19200, 128], P(('dp', 'ctx')), may hold values from -6 to 6
- mlp_flat: bfloat16 [57600, 128], P(('dp', 'ctx')), may hold values from -6 to 6
- norm_one: float32 [960], replicated, may hold values from 0.1 to 1.9
- norm_two: float32 [960], replicated, may hold values from 0.1 to 1.9
- cotangent: float32 [8, 512, 960], P('dp', 'ctx'), may hold values from -6 to 6
Outputs:
- block_out: float32 [8, 512, 960], P('dp', 'ctx')
- grad_in: float32 [8, 512, 960], P('dp', 'ctx')
- attn_grad: float32 [19200, 128], P(('dp', 'ctx'))
- mlp_grad: float32 [57600, 128], P(('dp', 'ctx'))
- norm_one_grad: float32 [960], replicated
- norm_two_grad: float32 [960], replicated
Inputs may be any that keep to these rules, and one draw needn't show every extreme that they name: `segments`: segment numbers never fall along a sequence; each document covers at most 256 positions, some document exactly that many.
All inputs are finite; a program needn't handle non-finite values.
Results may differ from a plain program's by a relative error of at most 0.015.
Values may be sent and summed in bfloat16 or wider, within the bound.
No kernel may reach another device: no remote copies, remote signals or barrier semaphores. Data moves between devices by JAX's collectives and lax.ppermute only.
A program may use at most 128 MiB of HBM per device.

v0:
```python
import jax
import jax.numpy as jnp
from jax import lax
from jax.sharding import PartitionSpec as P

D = 960
HEADS = 15
KV_HEADS = 5
HEAD_DIM = 64
FFN = 2560
EPS = 1e-05
THETA = 100000.0


def positions_of(segment_ids):
    earlier = (segment_ids[..., None, :] < segment_ids[..., :, None]).astype(jnp.int32)
    total_len = segment_ids.shape[-1]
    return jnp.arange(total_len, dtype=jnp.int32) - jnp.sum(earlier, axis=-1)


def rope_tables(positions):
    half_dim = HEAD_DIM // 2
    frequency = THETA ** (-2.0 * jnp.arange(half_dim, dtype=jnp.float32) / HEAD_DIM)
    angles = positions.astype(jnp.float32)[:, None] * frequency[None, :]
    return (jnp.cos(angles)[:, None, :], jnp.sin(angles)[:, None, :])


def rotate(vectors, cosine_table, sine_table):
    half_dim = vectors.shape[-1] // 2
    lower_half = vectors[..., :half_dim]
    upper_half = vectors[..., half_dim:]
    return jnp.concatenate(
        [
            lower_half * cosine_table - upper_half * sine_table,
            upper_half * cosine_table + lower_half * sine_table,
        ],
        axis=-1,
    )


def unrotate(grad_rows, cosine_table, sine_table):
    half_dim = grad_rows.shape[-1] // 2
    lower_half = grad_rows[..., :half_dim]
    upper_half = grad_rows[..., half_dim:]
    return jnp.concatenate(
        [
            lower_half * cosine_table + upper_half * sine_table,
            upper_half * cosine_table - lower_half * sine_table,
        ],
        axis=-1,
    )


def unpack_blocks(flat_rows, shapes, dp_count, ctx_count):
    pieces = flat_rows.reshape(dp_count, ctx_count, -1).transpose(1, 0, 2).reshape(ctx_count, -1)
    matrices = []
    offset = 0
    for height, width_cols in shapes:
        length = height * width_cols // ctx_count
        matrices.append(pieces[:, offset : offset + length].reshape(height, width_cols))
        offset = offset + length
    return matrices


def norm_forward(residual, gain_vec):
    inverse = lax.rsqrt(jnp.mean(residual * residual, axis=-1, keepdims=True) + EPS)
    return (inverse, residual * inverse * gain_vec)


def norm_backward(residual, inverse, gain_vec, grad_normed):
    scaled = grad_normed * gain_vec
    cubed = inverse * inverse * inverse
    grad_resid = inverse * scaled - residual * cubed * jnp.mean(
        scaled * residual, axis=-1, keepdims=True
    )
    grad_gain = jnp.sum(grad_normed * residual * inverse, axis=0)
    return (grad_resid, grad_gain)


def masked_scores(query_rot, key_whole, allowed, score_scale):
    scores = (
        jnp.einsum("sqkgd,slkd->skgql", query_rot, key_whole, preferred_element_type=jnp.float32)
        * score_scale
    )
    return jnp.where(allowed, scores, -jnp.inf)


def left_dot(left_cols, right_rows):
    return lax.dot_general(
        left_cols, right_rows, (((0,), (0,)), ((), ())), preferred_element_type=jnp.float32
    )


def body(hidden_in, segments, attn_flat, mlp_flat, norm_one, norm_two, cotangent):
    seq_count, local_len, model_width = hidden_in.shape
    seq_len = segments.shape[1]
    row_count = seq_count * local_len
    groups = HEADS // KV_HEADS
    qwidth = HEADS * HEAD_DIM
    kwidth = KV_HEADS * HEAD_DIM
    score_scale = HEAD_DIM ** (-0.5)
    low = jnp.bfloat16
    wide = jnp.float32
    dp_count = lax.axis_size("dp")
    ctx_count = lax.axis_size("ctx")
    attn_shapes = ((D, qwidth), (D, kwidth), (D, kwidth), (qwidth, D))
    mlp_shapes = ((D, FFN), (D, FFN), (FFN, D))
    start_row = lax.axis_index("ctx") * local_len
    attn_whole, mlp_whole = (
        lax.all_gather(attn_flat, ("dp", "ctx"), axis=0, tiled=True),
        lax.all_gather(mlp_flat, ("dp", "ctx"), axis=0, tiled=True),
    )
    w_query, w_key, w_value, w_out = unpack_blocks(attn_whole, attn_shapes, dp_count, ctx_count)
    w_gate, w_up, w_down = unpack_blocks(mlp_whole, mlp_shapes, dp_count, ctx_count)
    pos_all = positions_of(segments)
    pos_local = lax.dynamic_slice_in_dim(pos_all, start_row, local_len, 1)
    seg_local = lax.dynamic_slice_in_dim(segments, start_row, local_len, 1)
    cosine_table, sine_table = rope_tables(pos_local.reshape(-1))
    key_index = jnp.arange(seq_len, dtype=jnp.int32)
    query_index = start_row + jnp.arange(local_len, dtype=jnp.int32)
    allowed = (seg_local[:, :, None] == segments[:, None, :]) & (
        key_index[None, None, :] <= query_index[None, :, None]
    )
    allowed = allowed[:, None, None]
    residual = hidden_in.reshape(row_count, model_width)
    inv_one, normed_one = norm_forward(residual, norm_one)
    normed_one = normed_one.astype(low)
    query = jnp.dot(normed_one, w_query, preferred_element_type=wide).reshape(
        row_count, HEADS, HEAD_DIM
    )
    key_raw = jnp.dot(normed_one, w_key, preferred_element_type=wide).reshape(
        row_count, KV_HEADS, HEAD_DIM
    )
    value_low = jnp.dot(normed_one, w_value, preferred_element_type=wide).astype(low)
    query_rot = (
        rotate(query, cosine_table, sine_table)
        .astype(low)
        .reshape(seq_count, local_len, KV_HEADS, groups, HEAD_DIM)
    )
    key_rot = rotate(key_raw, cosine_table, sine_table).astype(low)
    kv_local = jnp.concatenate(
        [
            key_rot.reshape(seq_count, local_len, kwidth),
            value_low.reshape(seq_count, local_len, kwidth),
        ],
        axis=2,
    )
    kv_whole = lax.all_gather(kv_local, "ctx", axis=1, tiled=True)
    key_whole = kv_whole[:, :, :kwidth].reshape(seq_count, seq_len, KV_HEADS, HEAD_DIM)
    value_whole = kv_whole[:, :, kwidth:].reshape(seq_count, seq_len, KV_HEADS, HEAD_DIM)
    scores = masked_scores(query_rot, key_whole, allowed, score_scale)
    row_top = jnp.max(scores, axis=-1, keepdims=True)
    log_total = row_top + jnp.log(jnp.sum(jnp.exp(scores - row_top), axis=-1, keepdims=True))
    probs_low = jnp.exp(scores - log_total).astype(low)
    head_mix = jnp.einsum("skgql,slkd->sqkgd", probs_low, value_whole, preferred_element_type=wide)
    head_mix = head_mix.reshape(row_count, qwidth).astype(low)
    middle = residual + jnp.dot(head_mix, w_out, preferred_element_type=wide)
    inv_two, normed_two = norm_forward(middle, norm_two)
    normed_two = normed_two.astype(low)
    gate_pre = jnp.dot(normed_two, w_gate, preferred_element_type=wide)
    up_proj = jnp.dot(normed_two, w_up, preferred_element_type=wide)
    gate_sigmoid = jax.nn.sigmoid(gate_pre)
    active = (gate_pre * gate_sigmoid * up_proj).astype(low)
    block_rows = middle + jnp.dot(active, w_down, preferred_element_type=wide)
    one_cols, mix_cols, two_cols, active_cols = (
        lax.all_to_all(normed_one, "ctx", split_axis=1, concat_axis=0, tiled=True),
        lax.all_to_all(head_mix, "ctx", split_axis=1, concat_axis=0, tiled=True),
        lax.all_to_all(normed_two, "ctx", split_axis=1, concat_axis=0, tiled=True),
        lax.all_to_all(active, "ctx", split_axis=1, concat_axis=0, tiled=True),
    )
    cot_rows = cotangent.reshape(row_count, model_width)
    cot_low = cot_rows.astype(low)
    grad_active = jnp.dot(cot_low, w_down.T, preferred_element_type=wide)
    grad_gate = (
        grad_active * up_proj * gate_sigmoid * (1.0 + gate_pre * (1.0 - gate_sigmoid))
    ).astype(low)
    grad_up = (grad_active * gate_pre * gate_sigmoid).astype(low)
    grad_normed_two = jnp.dot(grad_gate, w_gate.T, preferred_element_type=wide) + jnp.dot(
        grad_up, w_up.T, preferred_element_type=wide
    )
    grad_middle, grad_gain_two = norm_backward(middle, inv_two, norm_two, grad_normed_two)
    grad_middle = cot_rows + grad_middle
    grad_mid_low = grad_middle.astype(low)
    grad_mix = jnp.dot(grad_mid_low, w_out.T, preferred_element_type=wide).astype(low)
    grad_mix = grad_mix.reshape(seq_count, local_len, KV_HEADS, groups, HEAD_DIM)
    attn_probs = jnp.exp(masked_scores(query_rot, key_whole, allowed, score_scale) - log_total)
    probs_low = attn_probs.astype(low)
    grad_probs = jnp.einsum("sqkgd,slkd->skgql", grad_mix, value_whole, preferred_element_type=wide)
    grad_value_all = jnp.einsum(
        "skgql,sqkgd->slkd", probs_low, grad_mix, preferred_element_type=wide
    )
    grad_scores = attn_probs * (
        grad_probs - jnp.sum(attn_probs * grad_probs, axis=-1, keepdims=True)
    )
    grad_scores_low = (grad_scores * score_scale).astype(low)
    grad_query = jnp.einsum(
        "skgql,slkd->sqkgd", grad_scores_low, key_whole, preferred_element_type=wide
    )
    grad_key_all = jnp.einsum(
        "skgql,sqkgd->slkd", grad_scores_low, query_rot, preferred_element_type=wide
    )
    kv_terms = jnp.concatenate(
        [
            grad_key_all.reshape(seq_count, seq_len, kwidth),
            grad_value_all.reshape(seq_count, seq_len, kwidth),
        ],
        axis=2,
    )
    kv_owned = lax.psum_scatter(
        kv_terms.astype(jnp.bfloat16), "ctx", scatter_dimension=1, tiled=True
    ).astype(jnp.float32)
    grad_key = kv_owned[:, :, :kwidth].reshape(row_count, KV_HEADS, HEAD_DIM)
    grad_value = kv_owned[:, :, kwidth:].reshape(row_count, kwidth).astype(low)
    grad_query = (
        unrotate(grad_query.reshape(row_count, HEADS, HEAD_DIM), cosine_table, sine_table)
        .reshape(row_count, qwidth)
        .astype(low)
    )
    grad_key = unrotate(grad_key, cosine_table, sine_table).reshape(row_count, kwidth).astype(low)
    grad_normed_one = (
        jnp.dot(grad_query, w_query.T, preferred_element_type=wide)
        + jnp.dot(grad_key, w_key.T, preferred_element_type=wide)
        + jnp.dot(grad_value, w_value.T, preferred_element_type=wide)
    )
    grad_resid, grad_gain_one = norm_backward(residual, inv_one, norm_one, grad_normed_one)
    grad_resid = grad_middle + grad_resid
    gathered = (
        lax.all_gather(grad_query, "ctx", axis=0, tiled=True),
        lax.all_gather(grad_key, "ctx", axis=0, tiled=True),
        lax.all_gather(grad_value, "ctx", axis=0, tiled=True),
        lax.all_gather(grad_mid_low, "ctx", axis=0, tiled=True),
        lax.all_gather(grad_gate, "ctx", axis=0, tiled=True),
        lax.all_gather(grad_up, "ctx", axis=0, tiled=True),
        lax.all_gather(cot_low, "ctx", axis=0, tiled=True),
    )
    all_query, all_key, all_value, all_mid, all_gate, all_up, all_cot = gathered
    attn_terms = jnp.concatenate(
        [
            left_dot(one_cols, all_query).reshape(-1),
            left_dot(one_cols, all_key).reshape(-1),
            left_dot(one_cols, all_value).reshape(-1),
            left_dot(mix_cols, all_mid).reshape(-1),
        ]
    ).reshape(-1, 128)
    mlp_terms = jnp.concatenate(
        [
            left_dot(two_cols, all_gate).reshape(-1),
            left_dot(two_cols, all_up).reshape(-1),
            left_dot(active_cols, all_cot).reshape(-1),
        ]
    ).reshape(-1, 128)
    attn_grad, mlp_grad = (
        lax.psum_scatter(
            attn_terms.astype(jnp.bfloat16), "dp", scatter_dimension=0, tiled=True
        ).astype(jnp.float32),
        lax.psum_scatter(
            mlp_terms.astype(jnp.bfloat16), "dp", scatter_dimension=0, tiled=True
        ).astype(jnp.float32),
    )
    gain_sums = lax.psum(jnp.stack([grad_gain_one, grad_gain_two]), ("dp", "ctx"))
    return (
        block_rows.reshape(seq_count, local_len, model_width),
        grad_resid.reshape(seq_count, local_len, model_width),
        attn_grad,
        mlp_grad,
        gain_sums[0],
        gain_sums[1],
    )


def solution(mesh):
    in_specs = (
        P("dp", "ctx", None),
        P("dp", None),
        P(("dp", "ctx"), None),
        P(("dp", "ctx"), None),
        P(),
        P(),
        P("dp", "ctx", None),
    )
    out_specs = (
        P("dp", "ctx", None),
        P("dp", "ctx", None),
        P(("dp", "ctx"), None),
        P(("dp", "ctx"), None),
        P(),
        P(),
    )
    return jax.shard_map(body, mesh=mesh, in_specs=in_specs, out_specs=out_specs, check_vma=False)
```

profile of v0, /device:TPU:0, one launch (start us, length us, event | category | flops | bytes accessed | tf_op | source)
XLA Modules:
  0.0 637.0 jit_solution(12020990512070765392)
XLA Ops:
  14.3 63.6 %all-gather.6.cloned.1.call-done = bf16[19200,128]{1,0:T(8,128)(2,1)} async-done(((bf16[600,128]{1,0:T(8,128)(2,1)}), bf16[19200,128]{1,0:T(8,128)(2,1)}) %all-gather.6.cloned.1.call-update) | async-done | bytes 4915216 | tf_op jit(solution)/shard_map/all_gather | solution.py:110
  77.9 7.6 %reshape.572 = bf16[8,4,76800]{2,1,0:T(4,128)(2,1)} reshape(bf16[19200,128]{1,0:T(8,128)(2,1)} %all-gather.6.cloned.1.call-done) | data formatting | bytes 9830400 | tf_op jit(solution)/shard_map/reshape | solution.py:55
  85.5 3.7 fusion.52
  97.1 4.5 reshape.581
  116.1 26.2 %all_gather.31 = bf16[1,512,640]{1,2,0:T(8,128)(2,1)S(1)} all-gather(bf16[1,128,640]{1,2,0:T(8,128)(2,1)S(1)} %pad_maximum_fusion.3), channel_id=1, replica_groups=mesh['dp'=8,'ctx'=4] {'ctx'}, dimensions={1}, use_global_device_ids=true | all-gather | bytes 819200 | tf_op jit(solution)/shard_map/all_gather | solution.py:148
  151.4 41.2 %all-gather.8.cloned.1.call-done = bf16[57600,128]{1,0:T(8,128)(2,1)} async-done(((bf16[1800,128]{1,0:T(8,128)(2,1)}), bf16[57600,128]{1,0:T(8,128)(2,1)}) %all-gather.8.cloned.1.call-update) | async-done | bytes 14745616 | tf_op jit(solution)/shard_map/all_gather | solution.py:111
  192.7 14.8 %reshape.582 = bf16[8,4,230400]{2,1,0:T(4,128)(2,1)} reshape(bf16[57600,128]{1,0:T(8,128)(2,1)} %all-gather.8.cloned.1.call-done) | data formatting | bytes 29491200 | tf_op jit(solution)/shard_map/reshape | solution.py:55
  207.4 13.3 %fusion.51 = (bf16[4,614400]{1,0:T(4,128)(2,1)}, bf16[4,614400]{1,0:T(4,128)(2,1)}, bf16[4,614400]{1,0:T(4,128)(2,1)}) fusion(bf16[4,1843200]{1,0:T(4,128)(2,1)} %bitcast.241), kind=kLoop, calls=%fused_computation.122 | loop fusion | bytes 29491200 | tf_op jit(solution)/shard_map/slice | solution.py:60
  220.7 9.6 %reshape.614 = bf16[2457600]{0:T(1024)(128)(2,1)} reshape(bf16[4,614400]{1,0:T(4,128)(2,1)} %get-tuple-element.12) | data formatting | bytes 9830400
  230.2 9.7 %reshape.586 = bf16[2560,960]{1,0:T(8,128)(2,1)} reshape(bf16[2457600]{0:T(1024)(128)(2,1)} %reshape.614) | data formatting | bytes 9830400 | tf_op jit(solution)/shard_map/reshape | solution.py:60
  239.9 9.2 %reshape.585 = bf16[960,2560]{1,0:T(8,128)(2,1)} reshape(bf16[4,614400]{1,0:T(4,128)(2,1)} %get-tuple-element.13) | data formatting | bytes 9830400 | tf_op jit(solution)/shard_map/reshape | solution.py:60
  249.1 9.2 %reshape.584 = bf16[960,2560]{1,0:T(8,128)(2,1)} reshape(bf16[4,614400]{1,0:T(4,128)(2,1)} %get-tuple-element.14) | data formatting | bytes 9830400 | tf_op jit(solution)/shard_map/reshape | solution.py:60
  264.5 3.9 multiply_convert_fusion
  268.4 4.1 fusion.60
  272.6 4.3 multiply_reduce_fusion
  285.1 3.7 copy.78
  293.8 31.8 %all_gather.39 = bf16[512,960]{0,1:T(8,128)(2,1)} all-gather(bf16[128,960]{0,1:T(8,128)(2,1)S(1)} %bitcast_convert_fusion), channel_id=1, replica_groups=mesh['dp'=8,'ctx'=4] {'ctx'}, dimensions={0}, use_global_device_ids=true | all-gather | bytes 1228800 | tf_op jit(solution)/shard_map/all_gather | solution.py:234
  329.6 49.0 %all_gather.36 = bf16[512,960]{0,1:T(8,128)(2,1)} all-gather(bf16[128,960]{0,1:T(8,128)(2,1)S(1)} %copy-done.20), channel_id=1, replica_groups=mesh['dp'=8,'ctx'=4] {'ctx'}, dimensions={0}, use_global_device_ids=true | all-gather | bytes 1228800 | tf_op jit(solution)/shard_map/all_gather | solution.py:231
  378.6 15.8 %all-to-all-start = ((bf16[128,4,240]{0,2,1:T(8,128)(2,1)}), bf16[128,4,240]{0,2,1:T(8,128)(2,1)S(1)}, u32[]{:S(2)}, u32[]{:S(2)}) async-start(bf16[128,4,240]{0,2,1:T(8,128)(2,1)} %multiply_convert_fusion.3), calls=%async_computation | async-start | bytes 491520 | tf_op jit(solution)/shard_map/all_to_all | solution.py:166
  404.2 5.1 all-to-all-start.3
  410.5 58.9 %all_gather.33 = bf16[512,960]{0,1:T(8,128)(2,1)S(1)} all-gather(bf16[128,960]{0,1:T(8,128)(2,1)S(1)} %bitcast.259), channel_id=1, replica_groups=mesh['dp'=8,'ctx'=4] {'ctx'}, dimensions={0}, use_global_device_ids=true | all-gather | bytes 1228800 | tf_op jit(solution)/shard_map/all_gather | solution.py:228
  473.0 12.6 %all-to-all-start.2 = ((bf16[128,4,240]{0,2,1:T(8,128)(2,1)}), bf16[128,4,240]{0,2,1:T(8,128)(2,1)S(1)}, u32[]{:S(2)}, u32[]{:S(2)}) async-start(bf16[128,4,240]{0,2,1:T(8,128)(2,1)} %bitcast.72), calls=%async_computation.2 | async-start | bytes 491520 | tf_op jit(solution)/shard_map/all_to_all | solution.py:168
  491.5 3.8 concatenate.68
  502.0 14.0 %all_gather.34 = bf16[512,320]{0,1:T(8,128)(2,1)S(1)} all-gather(bf16[128,320]{0,1:T(8,128)(2,1)S(1)} %bitcast.270), channel_id=1, replica_groups=mesh['dp'=8,'ctx'=4] {'ctx'}, dimensions={0}, use_global_device_ids=true | all-gather | bytes 409600 | tf_op jit(solution)/shard_map/all_gather | solution.py:229
  520.4 13.2 %all-gather = bf16[1,512,320]{1,2,0:T(8,128)(2,1)S(1)} all-gather(bf16[1,128,320]{1,2,0:T(8,128)(2,1)} %slice.122), channel_id=2, replica_groups=mesh['dp'=8,'ctx'=4] {'ctx'}, dimensions={1}, use_global_device_ids=true | all-gather | bytes 409600 | tf_op jit(solution)/shard_map/all_gather | solution.py:230
  542.7 3.7 convolution_convert_fusion.1
  546.4 3.8 concatenate.67
  550.2 3.7 concatenate.66
  553.9 6.0 pad_maximum_fusion
  559.9 5.3 fusion.9
  566.9 39.3 %psum.7 = f32[2,960]{1,0:T(2,128)S(1)} all-reduce(f32[2,960]{1,0:T(2,128)S(1)} %pad_maximum_fusion.7), channel_id=1, replica_groups=mesh['dp'=8,'ctx'=4] {'dp','ctx'}, use_global_device_ids=true, to_apply=%region_13.14 | all-reduce | flops 1920 | bytes 15360 | tf_op jit(solution)/shard_map/psum | solution.py:260
  609.5 18.5 %reduce-scatter.14.cloned.1.call-done = bf16[1800,128]{1,0:T(8,128)(2,1)} async-done(((bf16[14400,128]{1,0:T(8,128)(2,1)}), bf16[1800,128]{1,0:T(8,128)(2,1)}) %reduce-scatter.14.cloned.1.call-update) | async-done | bytes 460816
  (186 shorter events, 109.1 us)
Async XLA Ops:
  7.2 70.7 %all-gather.6.cloned.1.call-start = ((), (), s32[]{:S(2)}) async-start(), calls=%async_computation.7 | async-start | bytes 5068800 | tf_op jit(solution)/shard_map/all_gather | solution.py:110
  7.9 184.8 %all-gather.8.cloned.1.call-start = ((), (), s32[]{:S(2)}) async-start(), calls=%async_computation.8 | async-start | bytes 15206400 | tf_op jit(solution)/shard_map/all_gather | solution.py:111
  8.6 486.6 %reduce-scatter.10.cloned.1.call-start = ((), (), s32[]{:S(2)}) async-start(), calls=%async_computation.11 | async-start | bytes 819200
  10.4 75.1 %copy-start.33 = (f32[128]{0:T(128)}, f32[128]{0:T(128)S(1)}, u32[]{:S(2)}) copy-start(f32[128]{0:T(128)S(1)} %get-tuple-element.37) | copy-start | bytes 1540
  97.1 8.3 %copy-start.10 = (bf16[960,320]{1,0:T(8,128)(2,1)}, bf16[960,320]{1,0:T(8,128)(2,1)S(1)}, u32[]{:S(2)}) copy-start(bf16[960,320]{1,0:T(8,128)(2,1)S(1)} %reshape.574) | copy-start | bytes 1843204
  110.7 4.1 copy-start.12
  116.1 27.8 %copy-start.25 = (bf16[128,15,32]{0,2,1:T(8,128)(2,1)}, bf16[128,15,32]{0,2,1:T(8,128)(2,1)S(1)}, u32[]{:S(2)}) copy-start(bf16[128,15,32]{0,2,1:T(8,128)(2,1)S(1)} %get-tuple-element.26) | copy-start | bytes 368644
  116.1 27.8 %copy-start.27 = (bf16[128,15,32]{0,2,1:T(8,128)(2,1)}, bf16[128,15,32]{0,2,1:T(8,128)(2,1)S(1)}, u32[]{:S(2)}) copy-start(bf16[128,15,32]{0,2,1:T(8,128)(2,1)S(1)} %get-tuple-element.27) | copy-start | bytes 368644
  146.4 4.2 copy-start.32
  249.1 15.3 %slice-start = ((s8[5242880]{0:T(1024)(128)(4,1)}), s8[1048576]{0:T(1024)(128)(4,1)S(1)}, s32[]{:S(2)}) async-start(s8[5242880]{0:T(1024)(128)(4,1)} %bitcast.242), calls=%async_computation.14 | async-start | bytes 2097152
  258.3 6.1 slice-start.1
  272.5 4.4 copy-start.22
  272.6 4.4 copy-start.37
  272.6 6.1 copy-start.4
  285.1 6.6 %copy-start.31 = (f32[960]{0:T(1024)S(1)}, f32[960]{0:T(1024)}, u32[]{:S(2)}) copy-start(f32[960]{0:T(1024)} %param.11) | copy-start | bytes 11524
  285.1 7.8 %copy-start.34 = (f32[128]{0:T(128)S(1)}, f32[128]{0:T(128)}, u32[]{:S(2)}) copy-start(f32[128]{0:T(128)} %copy-done.33) | copy-start | bytes 1540
  291.1 38.5 %copy-start.20 = (bf16[128,960]{0,1:T(8,128)(2,1)S(1)}, bf16[128,960]{0,1:T(8,128)(2,1)}, u32[]{:S(2)}) copy-start(bf16[128,960]{0,1:T(8,128)(2,1)} %copy-done.19) | copy-start | bytes 737284
  291.2 247.9 %all-gather.12.cloned.1.call-start = ((), (), s32[]{:S(2)}) async-start(), calls=%async_computation.10 | async-start | bytes 3276800 | tf_op jit(solution)/shard_map/all_gather | solution.py:233
  325.6 53.0 %all-to-all-start.1 = ((bf16[128,4,240]{0,2,1:T(8,128)(2,1)}), bf16[128,4,240]{0,2,1:T(8,128)(2,1)S(1)}, u32[]{:S(2)}, u32[]{:S(2)}) async-start(bf16[128,4,240]{0,2,1:T(8,128)(2,1)} %bitcast.69), calls=%async_computation.1 | async-start | bytes 491520 | tf_op jit(solution)/shard_map/all_to_all | solution.py:167
  329.0 213.7 %all-gather.10.cloned.1.call-start = ((), (), s32[]{:S(2)}) async-start(), calls=%async_computation.9 | async-start | bytes 3276800 | tf_op jit(solution)/shard_map/all_gather | solution.py:232
  378.6 25.6 %all-to-all-start = ((bf16[128,4,240]{0,2,1:T(8,128)(2,1)}), bf16[128,4,240]{0,2,1:T(8,128)(2,1)S(1)}, u32[]{:S(2)}, u32[]{:S(2)}) async-start(bf16[128,4,240]{0,2,1:T(8,128)(2,1)} %multiply_convert_fusion.3), calls=%async_computation | async-start | bytes 491520 | tf_op jit(solution)/shard_map/all_to_all | solution.py:166
  404.2 68.8 %all-to-all-start.3 = ((bf16[128,4,640]{2,0,1:T(8,128)(2,1)}), bf16[128,4,640]{2,0,1:T(8,128)(2,1)}, u32[]{:S(2)}, u32[]{:S(2)}) async-start(bf16[128,4,640]{2,0,1:T(8,128)(2,1)} %bitcast.255), calls=%async_computation.3 | async-start | bytes 1310720 | tf_op jit(solution)/shard_map/all_to_all | solution.py:169
  410.4 62.5 %copy-start.17 = (bf16[128,15,64]{0,2,1:T(8,128)(2,1)}, bf16[128,15,64]{0,2,1:T(8,128)(2,1)S(1)}, u32[]{:S(2)}) copy-start(bf16[128,15,64]{0,2,1:T(8,128)(2,1)S(1)} %maximum_convert_fusion) | copy-start | bytes 737284
  473.0 66.1 %all-to-all-start.2 = ((bf16[128,4,240]{0,2,1:T(8,128)(2,1)}), bf16[128,4,240]{0,2,1:T(8,128)(2,1)S(1)}, u32[]{:S(2)}, u32[]{:S(2)}) async-start(bf16[128,4,240]{0,2,1:T(8,128)(2,1)} %bitcast.72), calls=%async_computation.2 | async-start | bytes 491520 | tf_op jit(solution)/shard_map/all_to_all | solution.py:168
  485.6 122.2 %reduce-scatter.12.cloned.1.call-start = ((), (), s32[]{:S(2)}) async-start(), calls=%async_computation.12 | async-start | bytes 1382400
  539.0 88.9 %reduce-scatter.14.cloned.1.call-start = ((), (), s32[]{:S(2)}) async-start(), calls=%async_computation.13 | async-start | bytes 4147200
  559.9 5.3 copy-start.13
  559.9 5.3 copy-start.24
  559.9 5.7 copy-start.11
  559.9 5.7 copy-start.30
  565.6 41.2 %copy-start.23 = (f32[128,960]{0,1:T(8,128)S(1)}, f32[128,960]{0,1:T(8,128)}, u32[]{:S(2)}) copy-start(f32[128,960]{0,1:T(8,128)} %get-tuple-element.11) | copy-start | bytes 1474564
  565.6 41.2 %copy-start.38 = (f32[128]{0:T(128)S(1)}, f32[128]{0:T(128)}, u32[]{:S(2)}) copy-start(f32[128]{0:T(128)} %get-tuple-element.36) | copy-start | bytes 1540
  (20 other events, 40.7 us)
Sparse Core Ops, SparseCore 0:
  10.8 66.9 all-gather.5
  80.7 111.8 all-gather.7
  291.3 28.9 reduce-scatter.9
  321.7 74.3 all-gather.11
  397.5 83.4 all-gather.9
  539.1 35.7 reduce-scatter.11
  578.4 49.5 reduce-scatter.13
where the time goes:
time: 646 us; the launch traced here: 637 us
  blocking collectives  232 us (36%)
  local copies, waits for them, and re-layouts  147 us (23%)
  waiting for transfers between devices  126 us (20%)
  matrix products  53.7 us (8%)
  starting transfers between devices  37.2 us (6%)
  other arithmetic  26 us (4%)
  between operations  15 us (2%)
    all_gather x1, waiting for transfers between devices, body(): lax.all_gather(attn_flat, ('dp', 'ctx'), axis=0, tiled=True)  63.6 us
    all_gather x1, blocking collectives, body(): lax.all_gather(grad_query, 'ctx', axis=0, tiled=True)  58.9 us
    all_gather x1, blocking collectives, body(): lax.all_gather(grad_mid_low, 'ctx', axis=0, tiled=True)  49 us
    all_gather x1, waiting for transfers between devices, body(): lax.all_gather(mlp_flat, ('dp', 'ctx'), axis=0, tiled=True)  41.2 us
    reshape x7, local copies, waits for them, and re-layouts, unpack_blocks(): pieces[:, offset:offset + length].reshape(height, width_cols)  40.4 us
    psum x1, blocking collectives, body(): lax.psum(jnp.stack([grad_gain_one, grad_gain_two]), ('dp', 'ctx'))  39.3 us
    all_gather x1, blocking collectives, body(): lax.all_gather(cot_low, 'ctx', axis=0, tiled=True)  31.8 us
    unnamed x89, local copies, waits for them, and re-layouts  31 us
  transfers between devices with their start and end apart: 11, of which 3 were waited for; matrix products, arithmetic and copies ran while one was open for 19% of the time, Pallas kernels for 0%

commit v1 on v0

--- a/solution.py
+++ b/solution.py
@@ -10,6 +10,27 @@
 FFN = 2560
 EPS = 1e-05
 THETA = 100000.0
+
+
+def gather_around(x, axis, dim):
+    size, index, width = (lax.axis_size(axis), lax.axis_index(axis), x.shape[dim])
+    right = [(i, (i + 1) % size) for i in range(size)]
+    backward = [(i, (i - 1) % size) for i in range(size)]
+    out = jnp.zeros((*x.shape[:dim], size * width, *x.shape[dim + 1 :]), x.dtype)
+    out = lax.dynamic_update_slice_in_dim(out, x, index * width, axis=dim)
+    from_left = from_right = x
+    half = size // 2
+    for step in range(1, half + 1):
+        from_left = lax.ppermute(from_left, axis, right)
+        out = lax.dynamic_update_slice_in_dim(
+            out, from_left, (index - step) % size * width, axis=dim
+        )
+        if step < size - half:
+            from_right = lax.ppermute(from_right, axis, backward)
+            out = lax.dynamic_update_slice_in_dim(
+                out, from_right, (index + step) % size * width, axis=dim
+            )
+    return out
 
 
 def positions_of(segment_ids):
@@ -225,7 +246,7 @@
     grad_resid, grad_gain_one = norm_backward(residual, inv_one, norm_one, grad_normed_one)
     grad_resid = grad_middle + grad_resid
     gathered = (
-        lax.all_gather(grad_query, "ctx", axis=0, tiled=True),
+        gather_around(grad_query, "ctx", 0),
         lax.all_gather(grad_key, "ctx", axis=0, tiled=True),
         lax.all_gather(grad_value, "ctx", axis=0, tiled=True),
         lax.all_gather(grad_mid_low, "ctx", axis=0, tiled=True),

time: 646 us -> 626 us (0.969)
  blocking collectives: 232 us -> 184 us
  waiting for transfers between devices: 126 us -> 140 us
  starting transfers between devices: 37.2 us -> 45.1 us
    all_gather x1 -> x0, blocking collectives: 58.9 us -> none  [body(): lax.all_gather(grad_query, 'ctx', axis=0, tiled=True)]
    ppermute x0 -> x3, waiting for transfers between devices: none -> 15.7 us  [the longest x2 15.7 us: gather_around(): from_left = lax.ppermute(from_left, axis, right)]
    all_to_all x1, starting transfers between devices: 15.8 us -> 3.41 us  [body(): lax.all_to_all(normed_one, 'ctx', split_axis=1, concat_axis=0, tiled=True)]
    all_gather x1, blocking collectives: 49 us -> 60.4 us  [body(): lax.all_gather(grad_mid_low, 'ctx', axis=0, tiled=True)]
    all_to_all x1, starting transfers between devices: 12.6 us -> 21.6 us  [body(): lax.all_to_all(normed_two, 'ctx', split_axis=1, concat_axis=0, tiled=True)]
  transfers between devices with their start and end apart: 11 -> 14, of which waited for: 3 -> 4; matrix products, arithmetic and copies ran while one was open for 19% -> 21% of each run, Pallas kernels for 0% -> 0%
where the time goes in v1:
time: 626 us; the launch traced here: 617 us
  blocking collectives  184 us (29%)
  local copies, waits for them, and re-layouts  153 us (24%)
  waiting for transfers between devices  140 us (22%)
  matrix products  53.7 us (9%)
  starting transfers between devices  45.1 us (7%)
  other arithmetic  25.6 us (4%)
  between operations  15 us (2%)
    all_gather x1, waiting for transfers between devices, body(): lax.all_gather(attn_flat, ('dp', 'ctx'), axis=0, tiled=True)  63.6 us
    all_gather x1, blocking collectives, body(): lax.all_gather(grad_mid_low, 'ctx', axis=0, tiled=True)  60.4 us
    all_gather x1, waiting for transfers between devices, body(): lax.all_gather(mlp_flat, ('dp', 'ctx'), axis=0, tiled=True)  42.1 us
    reshape x7, local copies, waits for them, and re-layouts, unpack_blocks(): pieces[:, offset:offset + length].reshape(height, width_cols)  40.5 us
    psum x1, blocking collectives, body(): lax.psum(jnp.stack([grad_gain_one, grad_gain_two]), ('dp', 'ctx'))  38.6 us
    all_gather x1, blocking collectives, body(): lax.all_gather(cot_low, 'ctx', axis=0, tiled=True)  32.5 us
    unnamed x89, local copies, waits for them, and re-layouts  31.5 us
    all_gather x1, blocking collectives, body(): kv_whole = lax.all_gather(kv_local, 'ctx', axis=1, tiled=True)  26 us
  transfers between devices with their start and end apart: 14, of which 4 were waited for; matrix products, arithmetic and copies ran while one was open for 21% of the time, Pallas kernels for 0%

profile of v1, /device:TPU:0, one launch (start us, length us, event | category | flops | bytes accessed | tf_op | source)
XLA Modules:
  0.0 617.3 jit_solution(13771331285308366346)
XLA Ops:
  14.3 63.6 %all-gather.6.cloned.1.call-done = bf16[19200,128]{1,0:T(8,128)(2,1)} async-done(((bf16[600,128]{1,0:T(8,128)(2,1)}), bf16[19200,128]{1,0:T(8,128)(2,1)}) %all-gather.6.cloned.1.call-update) | async-done | bytes 4915216 | tf_op jit(solution)/shard_map/all_gather | solution.py:131
  77.9 7.6 %reshape.572 = bf16[8,4,76800]{2,1,0:T(4,128)(2,1)} reshape(bf16[19200,128]{1,0:T(8,128)(2,1)} %all-gather.6.cloned.1.call-done) | data formatting | bytes 9830400 | tf_op jit(solution)/shard_map/reshape | solution.py:76
  85.5 3.7 fusion.54
  97.1 4.6 reshape.581
  116.1 26.0 %all_gather.28 = bf16[1,512,640]{1,2,0:T(8,128)(2,1)S(1)} all-gather(bf16[1,128,640]{1,2,0:T(8,128)(2,1)S(1)} %pad_maximum_fusion.3), channel_id=1, replica_groups=mesh['dp'=8,'ctx'=4] {'ctx'}, dimensions={1}, use_global_device_ids=true | all-gather | bytes 819200 | tf_op jit(solution)/shard_map/all_gather | solution.py:169
  150.4 42.1 %all-gather.8.cloned.1.call-done = bf16[57600,128]{1,0:T(8,128)(2,1)} async-done(((bf16[1800,128]{1,0:T(8,128)(2,1)}), bf16[57600,128]{1,0:T(8,128)(2,1)}) %all-gather.8.cloned.1.call-update) | async-done | bytes 14745616 | tf_op jit(solution)/shard_map/all_gather | solution.py:132
  192.5 14.8 %reshape.582 = bf16[8,4,230400]{2,1,0:T(4,128)(2,1)} reshape(bf16[57600,128]{1,0:T(8,128)(2,1)} %all-gather.8.cloned.1.call-done) | data formatting | bytes 29491200 | tf_op jit(solution)/shard_map/reshape | solution.py:76
  207.3 13.3 %fusion.53 = (bf16[4,614400]{1,0:T(4,128)(2,1)}, bf16[4,614400]{1,0:T(4,128)(2,1)}, bf16[4,614400]{1,0:T(4,128)(2,1)}) fusion(bf16[4,1843200]{1,0:T(4,128)(2,1)} %bitcast.241), kind=kLoop, calls=%fused_computation.128 | loop fusion | bytes 29491200 | tf_op jit(solution)/shard_map/slice | solution.py:81
  220.5 9.6 %reshape.614 = bf16[2457600]{0:T(1024)(128)(2,1)} reshape(bf16[4,614400]{1,0:T(4,128)(2,1)} %get-tuple-element.12) | data formatting | bytes 9830400
  230.1 9.7 %reshape.586 = bf16[2560,960]{1,0:T(8,128)(2,1)} reshape(bf16[2457600]{0:T(1024)(128)(2,1)} %reshape.614) | data formatting | bytes 9830400 | tf_op jit(solution)/shard_map/reshape | solution.py:81
  239.8 9.2 %reshape.585 = bf16[960,2560]{1,0:T(8,128)(2,1)} reshape(bf16[4,614400]{1,0:T(4,128)(2,1)} %get-tuple-element.13) | data formatting | bytes 9830400 | tf_op jit(solution)/shard_map/reshape | solution.py:81
  249.0 9.2 %reshape.584 = bf16[960,2560]{1,0:T(8,128)(2,1)} reshape(bf16[4,614400]{1,0:T(4,128)(2,1)} %get-tuple-element.14) | data formatting | bytes 9830400 | tf_op jit(solution)/shard_map/reshape | solution.py:81
  264.4 3.9 multiply_convert_fusion
  268.3 4.1 fusion.62
  272.4 4.3 multiply_reduce_fusion
  285.0 3.7 copy.78
  297.1 32.5 %all_gather.35 = bf16[512,960]{0,1:T(8,128)(2,1)} all-gather(bf16[128,960]{0,1:T(8,128)(2,1)S(1)} %bitcast_convert_fusion), channel_id=1, replica_groups=mesh['dp'=8,'ctx'=4] {'ctx'}, dimensions={0}, use_global_device_ids=true | all-gather | bytes 1228800 | tf_op jit(solution)/shard_map/all_gather | solution.py:255
  337.3 5.2 all-to-all-start.1
  342.6 60.4 %all_gather.32 = bf16[512,960]{0,1:T(8,128)(2,1)} all-gather(bf16[128,960]{0,1:T(8,128)(2,1)S(1)} %copy-done.19), channel_id=1, replica_groups=mesh['dp'=8,'ctx'=4] {'ctx'}, dimensions={0}, use_global_device_ids=true | all-gather | bytes 1228800 | tf_op jit(solution)/shard_map/all_gather | solution.py:252
  402.9 8.8 %all-to-all-start.3 = ((bf16[128,4,640]{2,0,1:T(8,128)(2,1)}), bf16[128,4,640]{2,0,1:T(8,128)(2,1)}, u32[]{:S(2)}, u32[]{:S(2)}) async-start(bf16[128,4,640]{2,0,1:T(8,128)(2,1)} %bitcast.255), calls=%async_computation.3 | async-start | bytes 1310720 | tf_op jit(solution)/shard_map/all_to_all | solution.py:190
  424.9 15.7 %collective-permute-done.2 = bf16[128,960]{0,1:T(8,128)(2,1)S(1)} collective-permute-done((bf16[128,960]{0,1:T(8,128)(2,1)}, bf16[128,960]{0,1:T(8,128)(2,1)S(1)}, u32[]{:S(2)}, u32[]{:S(2)}) %collective-permute-start.2) | collective-permute-done | bytes 245792 | tf_op jit(solution)/shard_map/ppermute | solution.py:24
  446.2 21.6 %all-to-all-start.2 = ((bf16[128,4,240]{0,2,1:T(8,128)(2,1)}), bf16[128,4,240]{0,2,1:T(8,128)(2,1)S(1)}, u32[]{:S(2)}, u32[]{:S(2)}) async-start(bf16[128,4,240]{0,2,1:T(8,128)(2,1)} %bitcast.72), calls=%async_computation.2 | async-start | bytes 491520 | tf_op jit(solution)/shard_map/all_to_all | solution.py:189
  473.8 3.8 concatenate.68
  484.3 13.6 %all_gather.30 = bf16[512,320]{0,1:T(8,128)(2,1)S(1)} all-gather(bf16[128,320]{0,1:T(8,128)(2,1)S(1)} %bitcast.270), channel_id=1, replica_groups=mesh['dp'=8,'ctx'=4] {'ctx'}, dimensions={0}, use_global_device_ids=true | all-gather | bytes 409600 | tf_op jit(solution)/shard_map/all_gather | solution.py:250
  502.4 13.2 %all-gather = bf16[1,512,320]{1,2,0:T(8,128)(2,1)S(1)} all-gather(bf16[1,128,320]{1,2,0:T(8,128)(2,1)} %slice.122), channel_id=2, replica_groups=mesh['dp'=8,'ctx'=4] {'ctx'}, dimensions={1}, use_global_device_ids=true | all-gather | bytes 409600 | tf_op jit(solution)/shard_map/all_gather | solution.py:251
  524.7 3.7 convolution_convert_fusion.1
  528.4 3.8 concatenate.67
  532.1 3.7 concatenate.66
  535.8 6.0 pad_maximum_fusion
  541.9 5.4 fusion.9
  549.8 38.6 %psum.7 = f32[2,960]{1,0:T(2,128)S(1)} all-reduce(f32[2,960]{1,0:T(2,128)S(1)} %pad_maximum_fusion.7), channel_id=1, replica_groups=mesh['dp'=8,'ctx'=4] {'dp','ctx'}, use_global_device_ids=true, to_apply=%region_13.14 | all-reduce | flops 1920 | bytes 15360 | tf_op jit(solution)/shard_map/psum | solution.py:281
  591.6 16.7 %reduce-scatter.14.cloned.1.call-done = bf16[1800,128]{1,0:T(8,128)(2,1)} async-done(((bf16[14400,128]{1,0:T(8,128)(2,1)}), bf16[1800,128]{1,0:T(8,128)(2,1)}) %reduce-scatter.14.cloned.1.call-update) | async-done | bytes 460816
  (196 shorter events, 120.3 us)
Async XLA Ops:
  7.2 70.7 %all-gather.6.cloned.1.call-start = ((), (), s32[]{:S(2)}) async-start(), calls=%async_computation.7 | async-start | bytes 5068800 | tf_op jit(solution)/shard_map/all_gather | solution.py:131
  7.9 184.6 %all-gather.8.cloned.1.call-start = ((), (), s32[]{:S(2)}) async-start(), calls=%async_computation.8 | async-start | bytes 15206400 | tf_op jit(solution)/shard_map/all_gather | solution.py:132
  8.6 468.9 %reduce-scatter.10.cloned.1.call-start = ((), (), s32[]{:S(2)}) async-start(), calls=%async_computation.11 | async-start | bytes 819200
  10.4 75.1 %copy-start.33 = (f32[128]{0:T(128)}, f32[128]{0:T(128)S(1)}, u32[]{:S(2)}) copy-start(f32[128]{0:T(128)S(1)} %get-tuple-element.37) | copy-start | bytes 1540
  97.1 8.3 %copy-start.10 = (bf16[960,320]{1,0:T(8,128)(2,1)}, bf16[960,320]{1,0:T(8,128)(2,1)S(1)}, u32[]{:S(2)}) copy-start(bf16[960,320]{1,0:T(8,128)(2,1)S(1)} %reshape.574) | copy-start | bytes 1843204
  116.1 27.6 %copy-start.25 = (bf16[128,15,32]{0,2,1:T(8,128)(2,1)}, bf16[128,15,32]{0,2,1:T(8,128)(2,1)S(1)}, u32[]{:S(2)}) copy-start(bf16[128,15,32]{0,2,1:T(8,128)(2,1)S(1)} %get-tuple-element.26) | copy-start | bytes 368644
  116.1 27.6 %copy-start.27 = (bf16[128,15,32]{0,2,1:T(8,128)(2,1)}, bf16[128,15,32]{0,2,1:T(8,128)(2,1)S(1)}, u32[]{:S(2)}) copy-start(bf16[128,15,32]{0,2,1:T(8,128)(2,1)S(1)} %get-tuple-element.27) | copy-start | bytes 368644
  249.0 15.3 %slice-start = ((s8[5242880]{0:T(1024)(128)(4,1)}), s8[1048576]{0:T(1024)(128)(4,1)S(1)}, s32[]{:S(2)}) async-start(s8[5242880]{0:T(1024)(128)(4,1)} %bitcast.242), calls=%async_computation.14 | async-start | bytes 2097152
  258.2 6.1 slice-start.1
  272.4 4.4 copy-start.22
  272.4 6.1 copy-start.5
  285.0 6.6 %copy-start.31 = (f32[960]{0:T(1024)S(1)}, f32[960]{0:T(1024)}, u32[]{:S(2)}) copy-start(f32[960]{0:T(1024)} %param.11) | copy-start | bytes 11524
  285.0 6.7 %copy-start.34 = (f32[128]{0:T(128)S(1)}, f32[128]{0:T(128)}, u32[]{:S(2)}) copy-start(f32[128]{0:T(128)} %copy-done.33) | copy-start | bytes 1540
  291.0 230.1 %all-gather.12.cloned.1.call-start = ((), (), s32[]{:S(2)}) async-start(), calls=%async_computation.10 | async-start | bytes 3276800 | tf_op jit(solution)/shard_map/all_gather | solution.py:254
  292.5 44.8 %all-to-all-start = ((bf16[128,4,240]{0,2,1:T(8,128)(2,1)}), bf16[128,4,240]{0,2,1:T(8,128)(2,1)S(1)}, u32[]{:S(2)}, u32[]{:S(2)}) async-start(bf16[128,4,240]{0,2,1:T(8,128)(2,1)} %multiply_convert_fusion.3), calls=%async_computation | async-start | bytes 491520 | tf_op jit(solution)/shard_map/all_to_all | solution.py:187
  295.9 228.7 %all-gather.10.cloned.1.call-start = ((), (), s32[]{:S(2)}) async-start(), calls=%async_computation.9 | async-start | bytes 3276800 | tf_op jit(solution)/shard_map/all_gather | solution.py:253
  329.6 6.8 %copy-start.17 = (bf16[128,2560]{1,0:T(8,128)(2,1)S(1)}, bf16[128,2560]{1,0:T(8,128)(2,1)}, u32[]{:S(2)}) copy-start(bf16[128,2560]{1,0:T(8,128)(2,1)} %get-tuple-element.21) | copy-start | bytes 1966084
  329.6 12.9 %copy-start.19 = (bf16[128,960]{0,1:T(8,128)(2,1)S(1)}, bf16[128,960]{0,1:T(8,128)(2,1)}, u32[]{:S(2)}) copy-start(bf16[128,960]{0,1:T(8,128)(2,1)} %copy-done.18) | copy-start | bytes 737284
  332.6 90.6 %collective-permute-start.1 = (bf16[128,960]{0,1:T(8,128)(2,1)}, bf16[128,960]{0,1:T(8,128)(2,1)}, u32[]{:S(2)}, u32[]{:S(2)}) collective-permute-start(bf16[128,960]{0,1:T(8,128)(2,1)} %bitcast.50), channel_id=1, source_target_pairs={{0,3},{1,0},{2,1},{3,2},{4,7},{5,4},{6,5},{7,6},{8,11},{9,8},{10,9... | collective-permute-start | bytes 737288 | tf_op jit(solution)/shard_map/ppermute | solution.py:29
  333.0 81.3 %collective-permute-start = (bf16[128,960]{0,1:T(8,128)(2,1)}, bf16[128,960]{0,1:T(8,128)(2,1)}, u32[]{:S(2)}, u32[]{:S(2)}) collective-permute-start(bf16[128,960]{0,1:T(8,128)(2,1)} %bitcast.50), channel_id=1, source_target_pairs={{0,1},{1,2},{2,3},{3,0},{4,5},{5,6},{6,7},{7,4},{8,9},{9,10},{10,1... | collective-permute-start | bytes 737288 | tf_op jit(solution)/shard_map/ppermute | solution.py:24
  337.3 65.6 %all-to-all-start.1 = ((bf16[128,4,240]{0,2,1:T(8,128)(2,1)}), bf16[128,4,240]{0,2,1:T(8,128)(2,1)}, u32[]{:S(2)}, u32[]{:S(2)}) async-start(bf16[128,4,240]{0,2,1:T(8,128)(2,1)} %bitcast.260), calls=%async_computation.1 | async-start | bytes 491520 | tf_op jit(solution)/shard_map/all_to_all | solution.py:188
  402.9 43.2 %all-to-all-start.3 = ((bf16[128,4,640]{2,0,1:T(8,128)(2,1)}), bf16[128,4,640]{2,0,1:T(8,128)(2,1)}, u32[]{:S(2)}, u32[]{:S(2)}) async-start(bf16[128,4,640]{2,0,1:T(8,128)(2,1)} %bitcast.255), calls=%async_computation.3 | async-start | bytes 1310720 | tf_op jit(solution)/shard_map/all_to_all | solution.py:190
  414.4 26.2 %collective-permute-start.2 = (bf16[128,960]{0,1:T(8,128)(2,1)}, bf16[128,960]{0,1:T(8,128)(2,1)S(1)}, u32[]{:S(2)}, u32[]{:S(2)}) collective-permute-start(bf16[128,960]{0,1:T(8,128)(2,1)} %collective-permute-done), channel_id=1, source_target_pairs={{0,1},{1,2},{2,3},{3,0},{4,5},{5,6},{6,7},{7,4},{8,9},{9,10},{10,1... | collective-permute-start | bytes 737288 | tf_op jit(solution)/shard_map/ppermute | solution.py:24
  446.2 74.9 %all-to-all-start.2 = ((bf16[128,4,240]{0,2,1:T(8,128)(2,1)}), bf16[128,4,240]{0,2,1:T(8,128)(2,1)S(1)}, u32[]{:S(2)}, u32[]{:S(2)}) async-start(bf16[128,4,240]{0,2,1:T(8,128)(2,1)} %bitcast.72), calls=%async_computation.2 | async-start | bytes 491520 | tf_op jit(solution)/shard_map/all_to_all | solution.py:189
  467.8 122.2 %reduce-scatter.12.cloned.1.call-start = ((), (), s32[]{:S(2)}) async-start(), calls=%async_computation.12 | async-start | bytes 1382400
  521.0 87.3 %reduce-scatter.14.cloned.1.call-start = ((), (), s32[]{:S(2)}) async-start(), calls=%async_computation.13 | async-start | bytes 4147200
  541.9 5.4 copy-start.13
  541.9 5.4 copy-start.24
  541.9 5.7 copy-start.11
  541.9 5.7 copy-start.30
  547.6 41.3 %copy-start.23 = (f32[128,960]{0,1:T(8,128)S(1)}, f32[128,960]{0,1:T(8,128)}, u32[]{:S(2)}) copy-start(f32[128,960]{0,1:T(8,128)} %get-tuple-element.11) | copy-start | bytes 1474564
  547.7 41.3 %copy-start.38 = (f32[128]{0:T(128)S(1)}, f32[128]{0:T(128)}, u32[]{:S(2)}) copy-start(f32[128]{0:T(128)} %get-tuple-element.36) | copy-start | bytes 1540
  (23 other events, 53.6 us)
Sparse Core Ops, SparseCore 0:
  10.8 66.9 all-gather.5
  80.7 111.7 all-gather.7
  291.1 27.5 reduce-scatter.9
  320.1 92.6 all-gather.11
  414.2 69.5 all-gather.9
  521.1 33.7 reduce-scatter.11
  558.4 49.8 reduce-scatter.13
